TPU v7x, 32 devices: a whole 2x2x4 slice. The times are simulated.
32 devices in a mesh: dp: 8 (over y, x, core), tensor: 4 (over z).
Axes of the slice: x: 2, y: 2, z: 4, core: 2. Of those that a mesh axis runs over, the one named last changes fastest.
Arguments:
- activations: bfloat16 [4096, 4096], P('dp'), may hold values from -1000 to 1000
- norm_gain: bfloat16 [4096], replicated, may hold values from 0.5 to 1.5
- query_blocks: bfloat16 [128, 32, 4096], P('dp', None, 'tensor'), may hold values from -64 to 64
- query_scales: int32 [128, 1, 4096], P('dp', None, 'tensor'), may hold values from -9 to -5
- key_blocks: bfloat16 [128, 32, 512], P('dp', None, 'tensor'), may hold values from -64 to 64
- key_scales: int32 [128, 1, 512], P('dp', None, 'tensor'), may hold values from -9 to -5
- value_blocks: bfloat16 [128, 32, 512], P('dp', None, 'tensor'), may hold values from -6 to 6
- value_scales: int32 [128, 1, 512], P('dp', None, 'tensor'), may hold values from -9 to -5
- output_blocks: bfloat16 [128, 32, 4096], P('tensor', None, 'dp'), may hold values from -6 to 6
- output_scales: int32 [128, 1, 4096], P('tensor', None, 'dp'), may hold values from -9 to -5
Outputs:
- attended: bfloat16 [4096, 4096], P('dp')
All inputs are finite; a program needn't handle non-finite values.
Results may differ from a plain program's by a relative error of at most 0.015.
The roundings to bfloat16 on the way count: a program that leaves them out, or rounds other values in their place, can miss the bound.
Values may be sent and summed in bfloat16 or wider, within the bound.
No kernel may reach another device: no remote copies, remote signals or barrier semaphores. Data moves between devices by JAX's collectives and lax.ppermute only.
A program may use at most 128 MiB of HBM per device.

v0:
```python
import math
import jax
import jax.numpy as jnp
from jax import lax
from jax.sharding import PartitionSpec as P

HEAD_DIM = 128
SEQ = 256
EPS = 1e-05
ROPE_BASE = 500000.0


def dequant(blocks, scales):
    factor = jnp.exp2(scales.astype(jnp.float32)).astype(blocks.dtype)
    weight = blocks * factor
    return weight.reshape(weight.shape[0] * weight.shape[1], weight.shape[2])


def rotate_pairs(states, positions):
    half_dim = states.shape[-1] // 2
    frequency = jnp.exp(
        -math.log(ROPE_BASE) * jnp.arange(half_dim, dtype=jnp.float32) * 2.0 / states.shape[-1]
    )
    angles = positions.astype(jnp.float32)[:, None] * frequency[None, :]
    cosine = jnp.cos(angles)[None, :, None, :]
    sine_part = jnp.sin(angles)[None, :, None, :]
    first = states[..., :half_dim]
    second = states[..., half_dim:]
    return jnp.concatenate(
        [first * cosine - second * sine_part, second * cosine + first * sine_part], axis=-1
    )


def attend(query_states, key_states, value_states, kv_count):
    tokens_here = query_states.shape[0]
    count = tokens_here // SEQ
    positions = jnp.arange(SEQ, dtype=jnp.int32)
    queries = rotate_pairs(query_states.reshape(count, SEQ, -1, HEAD_DIM), positions).astype(
        jnp.bfloat16
    )
    rotated_keys = rotate_pairs(
        key_states.reshape(count, SEQ, kv_count, HEAD_DIM), positions
    ).astype(jnp.bfloat16)
    value_heads = value_states.astype(jnp.bfloat16).reshape(count, SEQ, kv_count, HEAD_DIM)
    group_size = queries.shape[2] // kv_count
    queries = queries.reshape(count, SEQ, kv_count, group_size, HEAD_DIM)
    scores = jnp.einsum(
        "sqkgd,stkd->skgqt", queries, rotated_keys, preferred_element_type=jnp.float32
    ) * HEAD_DIM ** (-0.5)
    visible = positions[:, None] >= positions[None, :]
    scores = jnp.where(visible, scores, -jnp.inf)
    attn_weights = jax.nn.softmax(scores, axis=-1).astype(jnp.bfloat16)
    context = jnp.einsum(
        "skgqt,stkd->sqkgd", attn_weights, value_heads, preferred_element_type=jnp.float32
    )
    return context.astype(jnp.bfloat16).reshape(tokens_here, -1)


def shards(
    activations,
    norm_gain,
    query_blocks,
    query_scales,
    key_blocks,
    key_scales,
    value_blocks,
    value_scales,
    output_blocks,
    output_scales,
):
    query_exps = query_scales.astype(jnp.bfloat16)
    key_exps = key_scales.astype(jnp.bfloat16)
    value_exps = value_scales.astype(jnp.bfloat16)
    output_exps = output_scales.astype(jnp.bfloat16)
    wide_rows = activations.astype(jnp.float32)
    inverse = lax.rsqrt(jnp.mean(wide_rows * wide_rows, axis=-1, keepdims=True) + EPS)
    normed = (wide_rows * inverse * norm_gain.astype(jnp.float32)).astype(jnp.bfloat16)

    def product(blocks, scales):
        return jnp.dot(normed, dequant(blocks, scales), preferred_element_type=jnp.float32)

    def add_one(pieces):
        return product(pieces[0], pieces[1])

    query_states = add_one(
        (
            lax.all_gather(query_blocks, "dp", axis=0, tiled=True),
            lax.all_gather(query_exps, "dp", axis=0, tiled=True),
        )
    )
    key_states = add_one(
        (
            lax.all_gather(key_blocks, "dp", axis=0, tiled=True),
            lax.all_gather(key_exps, "dp", axis=0, tiled=True),
        )
    )
    value_states = add_one(
        (
            lax.all_gather(value_blocks, "dp", axis=0, tiled=True),
            lax.all_gather(value_exps, "dp", axis=0, tiled=True),
        )
    )
    context = attend(query_states, key_states, value_states, key_blocks.shape[2] // HEAD_DIM)
    pieces = (
        lax.all_gather(output_blocks, "dp", axis=2, tiled=True),
        lax.all_gather(output_exps, "dp", axis=2, tiled=True),
    )
    block_out = jnp.dot(context, dequant(pieces[0], pieces[1]), preferred_element_type=jnp.float32)
    return lax.psum(block_out.astype(jnp.bfloat16), "tensor")


def solution(mesh):
    placed = (
        P("dp", None),
        P(),
        P("dp", None, "tensor"),
        P("dp", None, "tensor"),
        P("dp", None, "tensor"),
        P("dp", None, "tensor"),
        P("dp", None, "tensor"),
        P("dp", None, "tensor"),
        P("tensor", None, "dp"),
        P("tensor", None, "dp"),
    )
    return jax.shard_map(
        shards, mesh=mesh, in_specs=placed, out_specs=P("dp", None), check_vma=False
    )
```

profile of v0, /device:TPU:0, one launch (start us, length us, event | category | flops | bytes accessed | tf_op | source)
XLA Modules:
  0.0 358.5 jit_solution(17838992438456256269)
XLA Ops:
  10.2 0.9 convert_element_type.99
  11.8 0.9 convert_element_type.110
  12.7 12.4 %all_gather.31 = bf16[32,1,4096]{2,1,0:T(2,128)(2,1)S(1)} all-gather(bf16[32,1,512]{2,1,0:T(2,128)(2,1)S(1)} %convert_element_type.110), channel_id=1, replica_groups=mesh['dp'=8,'tensor'=4] {'dp'}, dimensions={2}, use_global_device_ids=true | all-gather | bytes 294912 | tf_op jit(solution)/shard_map/all_gather | solution.py:106
  25.1 0.9 exponential_convert_fusion
  26.4 9.1 %all_gather.27 = bf16[128,1,128]{2,0,1:T(8,128)(2,1)S(1)} all-gather(bf16[16,1,128]{2,0,1:T(8,128)(2,1)S(1)} %convert_element_type.99), channel_id=1, replica_groups=mesh['dp'=8,'tensor'=4] {'dp'}, dimensions={0}, use_global_device_ids=true | all-gather | bytes 36864 | tf_op jit(solution)/shard_map/all_gather | solution.py:94
  35.5 8.3 %all_gather.25 = bf16[128,1,128]{2,0,1:T(8,128)(2,1)S(1)} all-gather(bf16[16,1,128]{2,0,1:T(8,128)(2,1)S(1)} %convert_element_type.95), channel_id=1, replica_groups=mesh['dp'=8,'tensor'=4] {'dp'}, dimensions={0}, use_global_device_ids=true | all-gather | bytes 36864 | tf_op jit(solution)/shard_map/all_gather | solution.py:100
  43.8 9.4 %all_gather.29 = bf16[128,1,1024]{2,0,1:T(8,128)(2,1)S(1)} all-gather(bf16[16,1,1024]{2,0,1:T(8,128)(2,1)S(1)} %copy_convert_fusion), channel_id=1, replica_groups=mesh['dp'=8,'tensor'=4] {'dp'}, dimensions={0}, use_global_device_ids=true | all-gather | bytes 294912 | tf_op jit(solution)/shard_map/all_gather | solution.py:88
  53.2 3.1 fusion
  56.8 3.6 %fusion.2 = bf16[512,4096]{1,0:T(8,128)(2,1)} fusion(bf16[512,4096]{1,0:T(8,128)(2,1)S(1)} %copy-done, f32[4096]{0:T(1024)S(1)} %convert_element_type.93, f32[512]{0:T(512)S(1)} %add_rsqrt_fusion), kind=kLoop, calls=%fused_computation.4 | loop fusion | flops 8388608 | bytes 8407040 | tf_op jit(solution)/shard_map/convert_element_type | solution.py:77
  60.4 1.3 broadcast_multiply_fusion.2
  61.8 3.7 %convolution_bitcast_fusion = f32[2,256,1,128]{1,3,0,2:T(8,128)S(1)} fusion(bf16[2,256,4096]{2,1,0:T(8,128)(2,1)} %bitcast.88, bf16[4096,128,1]{1,0,2:T(8,128)(2,1)S(1)} %bitcast.92), kind=kOutput, calls=%fused_computation.18 | convolution fusion | flops 536870912 | bytes 5505024 | tf_op jit(solution)/shard_map/dot_general | solution.py:80
  65.5 1.3 broadcast_multiply_fusion.3
  66.8 3.4 convolution_convert_fusion.1
  70.3 47.6 %all-gather.9.cloned.1.call-done = bf16[128,32,1024]{2,1,0:T(8,128)(2,1)} async-done(((bf16[16,32,1024]{2,1,0:T(8,128)(2,1)}), bf16[128,32,1024]{2,1,0:T(8,128)(2,1)}) %all-gather.9.cloned.1.call-update) | async-done | bytes 8388624 | tf_op jit(solution)/shard_map/all_gather | solution.py:87
  117.9 7.2 %broadcast_multiply_fusion.1 = bf16[128,32,1024]{2,1,0:T(8,128)(2,1)} fusion(bf16[128,32,1024]{2,1,0:T(8,128)(2,1)} %all-gather.9.cloned.1.call-done, bf16[128,1024]{1,0:T(8,128)(2,1)S(1)} %fusion.20), kind=kLoop, calls=%fused_computation.10 | loop fusion | flops 4194304 | bytes 17039360 | tf_op jit(solution)/shard_map/mul | solution.py:15
  125.1 12.1 %copy.28 = bf16[1024,4096]{1,0:T(8,128)(2,1)} copy(bf16[1024,4096]{0,1:T(8,128)(2,1)} %bitcast.87) | data formatting | bytes 16777216 | tf_op jit(solution)/shard_map/dot_general | solution.py:80
  137.2 8.2 %fusion.30 = f32[2,256,8,128]{1,3,2,0:T(8,128)S(1)} fusion(bf16[2,256,4096,1]{2,1,3,0:T(8,128)(2,1)} %bitcast.89, bf16[8,128,4096,1]{2,1,0,3:T(8,128)(2,1)} %bitcast.91), kind=kOutput, calls=%fused_computation.55 | convolution fusion | flops 4294967296 | bytes 14680064 | tf_op jit(solution)/shard_map/dot_general | solution.py:80
  146.6 0.9 fusion.3
  147.5 1.3 fusion.11
  149.5 26.0 %all-gather.11.cloned.1.call-done = bf16[32,32,4096]{2,1,0:T(8,128)(2,1)} async-done(((bf16[32,32,512]{2,1,0:T(8,128)(2,1)}), bf16[32,32,4096]{2,1,0:T(8,128)(2,1)}) %all-gather.11.cloned.1.call-update) | async-done | bytes 8388624 | tf_op jit(solution)/shard_map/all_gather | solution.py:105
  175.5 7.3 %broadcast_multiply_fusion = bf16[32,32,4096]{2,1,0:T(8,128)(2,1)} fusion(bf16[32,32,4096]{2,1,0:T(8,128)(2,1)} %all-gather.11.cloned.1.call-done, bf16[32,4096]{1,0:T(8,128)(2,1)S(1)} %bitcast.93), kind=kLoop, calls=%fused_computation.7 | loop fusion | flops 4194304 | bytes 17039360 | tf_op jit(solution)/shard_map/mul | solution.py:15
  182.8 9.4 %convolution_convert_fusion = bf16[512,4096]{1,0:T(8,128)(2,1)} fusion(bf16[1024,4096]{1,0:T(8,128)(2,1)} %bitcast.90, bf16[64,8,8,128]{3,2,1,0:T(8,128)(2,1)S(1)} %bitcast.94), kind=kOutput, calls=%fused_computation.5 | convolution fusion | flops 4297064448 | bytes 13631488 | tf_op jit(solution)/shard_map/dot_general | solution.py:108
  192.2 155.1 %all-reduce.2.cloned.1.call-done = bf16[512,4096]{1,0:T(8,128)(2,1)} async-done(((bf16[512,4096]{1,0:T(8,128)(2,1)}), bf16[512,4096]{1,0:T(8,128)(2,1)}) %all-reduce.2.cloned.1.call-update) | async-done | bytes 4194320 | tf_op jit(solution)/shard_map/psum | solution.py:109
  347.3 4.7 %copy.55 = bf16[512,4096]{1,0:T(8,128)(2,1)} copy(bf16[512,4096]{1,0:T(8,128)(2,1)} %all-reduce.2.cloned.1.call-done) | data formatting | bytes 8388608
  (32 shorter events, 7.1 us)
Async XLA Ops:
  6.5 37.2 %copy-start.1 = (s32[16,1,1024]{2,1,0:T(1,128)S(1)}, s32[16,1,1024]{2,1,0:T(1,128)}, u32[]{:S(2)}) copy-start(s32[16,1,1024]{2,1,0:T(1,128)} %param.13) | copy-start | bytes 196612
  6.5 53.9 %all-gather.7.cloned.1.call-start = ((), (), s32[]{:S(2)}) async-start(), calls=%async_computation.1 | async-start | bytes 1179648 | tf_op jit(solution)/shard_map/all_gather | solution.py:93
  7.3 58.3 %all-gather.5.cloned.1.call-start = ((), (), s32[]{:S(2)}) async-start(), calls=%async_computation | async-start | bytes 1179648 | tf_op jit(solution)/shard_map/all_gather | solution.py:99
  8.0 109.9 %all-gather.9.cloned.1.call-start = ((), (), s32[]{:S(2)}) async-start(), calls=%async_computation.2 | async-start | bytes 9437184 | tf_op jit(solution)/shard_map/all_gather | solution.py:87
  8.7 166.8 %all-gather.11.cloned.1.call-start = ((), (), s32[]{:S(2)}) async-start(), calls=%async_computation.3 | async-start | bytes 9437184 | tf_op jit(solution)/shard_map/all_gather | solution.py:105
  9.3 338.0 %all-reduce.2.cloned.1.call-start = ((), (), s32[]{:S(2)}) async-start(), calls=%async_computation.4 | async-start | bytes 8388608 | tf_op jit(solution)/shard_map/psum | solution.py:109
  9.4 47.4 %copy-start = (bf16[512,4096]{1,0:T(8,128)(2,1)S(1)}, bf16[512,4096]{1,0:T(8,128)(2,1)}, u32[]{:S(2)}) copy-start(bf16[512,4096]{1,0:T(8,128)(2,1)} %param.10) | copy-start | bytes 12582916
Sparse Core Ops, SparseCore 0:
  9.2 26.8 all-gather.6
  38.0 23.6 all-gather.4
  63.6 54.2 all-gather.8
  119.6 55.8 all-gather.10
  192.3 154.9 all-reduce.1
where the time goes:
time: 359 us
  waiting for transfers between devices  231 us (64%)
  blocking collectives  39.2 us (11%)
  other arithmetic  29.8 us (8%)
  matrix products  26.9 us (7%)
  local copies, waits for them, and re-layouts  17.9 us (5%)
  between operations  13.3 us (4%)
    psum x1, waiting for transfers between devices, shards(): return lax.psum(block_out.astype(jnp.bfloat16), 'tensor')  155 us
    all_gather x1, waiting for transfers between devices, shards(): lax.all_gather(query_blocks, 'dp', axis=0, tiled=True)  47.6 us
    all_gather x1, waiting for transfers between devices, shards(): lax.all_gather(output_blocks, 'dp', axis=2, tiled=True)  26 us
    mul x7, other arithmetic, dequant(): weight = blocks * factor  17.3 us
    dot_general x3, matrix products, product(): jnp.dot(normed, dequant(blocks, scales), preferred_element_type=jnp.float32)  15.4 us
    all_gather x1, blocking collectives, shards(): lax.all_gather(output_exps, 'dp', axis=2, tiled=True)  12.4 us
    dot_general x1, local copies, waits for them, and re-layouts, product(): jnp.dot(normed, dequant(blocks, scales), preferred_element_type=jnp.float32)  12.1 us
    all_gather x1, blocking collectives, shards(): lax.all_gather(query_exps, 'dp', axis=0, tiled=True)  9.4 us
  transfers between devices with their start and end apart: 5, of which 3 were waited for; matrix products, arithmetic and copies ran while one was open for 15% of the time, Pallas kernels for 0%

commit v1 on v0

--- a/solution.py
+++ b/solution.py
@@ -3,11 +3,17 @@
 import jax.numpy as jnp
 from jax import lax
 from jax.sharding import PartitionSpec as P
+from jax.lax import all_gather
 
 HEAD_DIM = 128
 SEQ = 256
 EPS = 1e-05
 ROPE_BASE = 500000.0
+
+
+def work_ways(incoming_x):
+    value_now = jnp.concatenate(all_gather(incoming_x, axis_name="dp"), 2)
+    return value_now
 
 
 def dequant(blocks, scales):
@@ -101,10 +107,7 @@
         )
     )
     context = attend(query_states, key_states, value_states, key_blocks.shape[2] // HEAD_DIM)
-    pieces = (
-        lax.all_gather(output_blocks, "dp", axis=2, tiled=True),
-        lax.all_gather(output_exps, "dp", axis=2, tiled=True),
-    )
+    pieces = (work_ways(output_blocks), lax.all_gather(output_exps, "dp", axis=2, tiled=True))
     block_out = jnp.dot(context, dequant(pieces[0], pieces[1]), preferred_element_type=jnp.float32)
     return lax.psum(block_out.astype(jnp.bfloat16), "tensor")
 

time: 359 us -> 374 us (1.042)
  local copies, waits for them, and re-layouts: 17.9 us -> 29.7 us
  other arithmetic: 29.8 us -> 34.8 us
    unnamed x6 -> x7, local copies, waits for them, and re-layouts: 5 us -> 17 us
    mul x7, other arithmetic: 17.3 us -> 21.2 us  [dequant(): weight = blocks * factor]
  transfers between devices with their start and end apart: 5 -> 5, of which waited for: 3 -> 3; matrix products, arithmetic and copies ran while one was open for 15% -> 14% of each run, Pallas kernels for 0% -> 0%
where the time goes in v1:
time: 374 us; the launch traced here: 373 us
  waiting for transfers between devices  229 us (61%)
  blocking collectives  39.2 us (10%)
  other arithmetic  34.8 us (9%)
  local copies, waits for them, and re-layouts  29.7 us (8%)
  matrix products  26.9 us (7%)
  between operations  13.3 us (4%)
    psum x1, waiting for transfers between devices, shards(): return lax.psum(block_out.astype(jnp.bfloat16), 'tensor')  155 us
    all_gather x1, waiting for transfers between devices, shards(): lax.all_gather(query_blocks, 'dp', axis=0, tiled=True)  46.9 us
    all_gather x1, waiting for transfers between devices, work_ways(): value_now = jnp.concatenate(all_gather(incoming_x, axis_name='dp'), 2)  24.5 us
    mul x7, other arithmetic, dequant(): weight = blocks * factor  21.2 us
    unnamed x7, local copies, waits for them, and re-layouts  17 us
    dot_general x3, matrix products, product(): jnp.dot(normed, dequant(blocks, scales), preferred_element_type=jnp.float32)  15.4 us
    all_gather x1, blocking collectives, shards(): lax.all_gather(output_exps, 'dp', axis=2, tiled=True)  12.4 us
    dot_general x1, local copies, waits for them, and re-layouts, product(): jnp.dot(normed, dequant(blocks, scales), preferred_element_type=jnp.float32)  12 us
  transfers between devices with their start and end apart: 5, of which 3 were waited for; matrix products, arithmetic and copies ran while one was open for 14% of the time, Pallas kernels for 0%

profile of v1, /device:TPU:0, one launch (start us, length us, event | category | flops | bytes accessed | tf_op | source)
XLA Modules:
  0.0 373.2 jit_solution(4274897284583856472)
XLA Ops:
  10.2 0.9 convert_element_type.99
  11.8 0.9 convert_element_type.110
  12.7 12.4 %all_gather.35 = bf16[32,1,4096]{2,1,0:T(2,128)(2,1)S(1)} all-gather(bf16[32,1,512]{2,1,0:T(2,128)(2,1)S(1)} %convert_element_type.110), channel_id=1, replica_groups=mesh['dp'=8,'tensor'=4] {'dp'}, dimensions={2}, use_global_device_ids=true | all-gather | bytes 294912 | tf_op jit(solution)/shard_map/all_gather | solution.py:110
  25.1 1.8 convert_reduce_fusion
  27.0 9.1 %all_gather.30 = bf16[128,1,128]{2,0,1:T(8,128)(2,1)S(1)} all-gather(bf16[16,1,128]{2,0,1:T(8,128)(2,1)S(1)} %convert_element_type.99), channel_id=1, replica_groups=mesh['dp'=8,'tensor'=4] {'dp'}, dimensions={0}, use_global_device_ids=true | all-gather | bytes 36864 | tf_op jit(solution)/shard_map/all_gather | solution.py:100
  36.1 8.2 %all_gather.28 = bf16[128,1,128]{2,0,1:T(8,128)(2,1)S(1)} all-gather(bf16[16,1,128]{2,0,1:T(8,128)(2,1)S(1)} %convert_element_type.95), channel_id=1, replica_groups=mesh['dp'=8,'tensor'=4] {'dp'}, dimensions={0}, use_global_device_ids=true | all-gather | bytes 36864 | tf_op jit(solution)/shard_map/all_gather | solution.py:106
  44.4 9.4 %all_gather.32 = bf16[128,1,1024]{2,0,1:T(8,128)(2,1)S(1)} all-gather(bf16[16,1,1024]{2,0,1:T(8,128)(2,1)S(1)} %copy_convert_fusion), channel_id=1, replica_groups=mesh['dp'=8,'tensor'=4] {'dp'}, dimensions={0}, use_global_device_ids=true | all-gather | bytes 294912 | tf_op jit(solution)/shard_map/all_gather | solution.py:94
  53.8 3.3 fusion
  57.6 3.6 fusion.2
  61.2 1.3 broadcast_multiply_fusion.1
  62.5 3.7 convolution_bitcast_fusion
  66.3 1.3 broadcast_multiply_fusion.2
  67.6 3.4 convolution_convert_fusion.1
  71.1 46.9 %all-gather.10.cloned.1.call-done = bf16[128,32,1024]{2,1,0:T(8,128)(2,1)} async-done(((bf16[16,32,1024]{2,1,0:T(8,128)(2,1)}), bf16[128,32,1024]{2,1,0:T(8,128)(2,1)}) %all-gather.10.cloned.1.call-update) | async-done | bytes 8388624 | tf_op jit(solution)/shard_map/all_gather | solution.py:93
  117.9 7.2 %broadcast_multiply_fusion = bf16[128,32,1024]{2,1,0:T(8,128)(2,1)} fusion(bf16[128,32,1024]{2,1,0:T(8,128)(2,1)} %all-gather.10.cloned.1.call-done, bf16[128,1024]{1,0:T(8,128)(2,1)S(1)} %fusion.20), kind=kLoop, calls=%fused_computation.10 | loop fusion | flops 4194304 | bytes 17039360 | tf_op jit(solution)/shard_map/mul | solution.py:21
  125.2 12.0 %copy.30 = bf16[1024,4096]{1,0:T(8,128)(2,1)} copy(bf16[1024,4096]{0,1:T(8,128)(2,1)} %bitcast.91) | data formatting | bytes 16777216 | tf_op jit(solution)/shard_map/dot_general | solution.py:86
  137.1 8.2 %fusion.30 = f32[2,256,8,128]{1,3,2,0:T(8,128)S(1)} fusion(bf16[2,256,4096,1]{2,1,3,0:T(8,128)(2,1)} %bitcast.94, bf16[8,128,4096,1]{2,1,0,3:T(8,128)(2,1)} %bitcast.96), kind=kOutput, calls=%fused_computation.54 | convolution fusion | flops 4294967296 | bytes 14680064 | tf_op jit(solution)/shard_map/dot_general | solution.py:86
  147.4 1.3 fusion.11
  149.5 24.5 %all-gather.12.cloned.1.call-done = bf16[256,32,512]{2,1,0:T(8,128)(2,1)} async-done(((bf16[32,32,512]{2,1,0:T(8,128)(2,1)}), bf16[256,32,512]{2,1,0:T(8,128)(2,1)}) %all-gather.12.cloned.1.call-update) | async-done | bytes 8388624 | tf_op jit(solution)/shard_map/all_gather | solution.py:15
  174.0 11.2 %bitcast_multiply_fusion = bf16[32,32,8,512]{3,2,1,0:T(8,128)(2,1)} fusion(bf16[8,32,32,512]{3,2,1,0:T(8,128)(2,1)} %bitcast.95, bf16[32,8,512]{2,1,0:T(8,128)(2,1)S(1)} %bitcast.99), kind=kLoop, calls=%fused_computation.5 | loop fusion | flops 4194304 | bytes 17039360 | tf_op jit(solution)/shard_map/mul | solution.py:21
  185.2 12.2 %copy.50 = bf16[128,8,8,512]{3,1,2,0:T(8,128)(2,1)} copy(bf16[128,8,8,512]{3,2,1,0:T(8,128)(2,1)} %bitcast.92) | data formatting | bytes 16777216
  197.4 9.4 %convolution_convert_fusion = bf16[512,4096]{1,0:T(8,128)(2,1)} fusion(bf16[1024,4096]{1,0:T(8,128)(2,1)} %bitcast.97, bf16[64,8,8,128]{3,2,1,0:T(8,128)(2,1)S(1)} %bitcast.101), kind=kOutput, calls=%fused_computation.6 | convolution fusion | flops 4297064448 | bytes 13631488 | tf_op jit(solution)/shard_map/dot_general | solution.py:111
  206.8 155.1 %all-reduce.2.cloned.1.call-done = bf16[512,4096]{1,0:T(8,128)(2,1)} async-done(((bf16[512,4096]{1,0:T(8,128)(2,1)}), bf16[512,4096]{1,0:T(8,128)(2,1)}) %all-reduce.2.cloned.1.call-update) | async-done | bytes 4194320 | tf_op jit(solution)/shard_map/psum | solution.py:112
  361.9 4.7 %copy.58 = bf16[512,4096]{1,0:T(8,128)(2,1)} copy(bf16[512,4096]{1,0:T(8,128)(2,1)} %all-reduce.2.cloned.1.call-done) | data formatting | bytes 8388608
  (33 shorter events, 7.8 us)
Async XLA Ops:
  6.5 37.8 %copy-start.1 = (s32[16,1,1024]{2,1,0:T(1,128)S(1)}, s32[16,1,1024]{2,1,0:T(1,128)}, u32[]{:S(2)}) copy-start(s32[16,1,1024]{2,1,0:T(1,128)} %param.13) | copy-start | bytes 196612
  6.5 54.7 %all-gather.8.cloned.1.call-start = ((), (), s32[]{:S(2)}) async-start(), calls=%async_computation.1 | async-start | bytes 1179648 | tf_op jit(solution)/shard_map/all_gather | solution.py:99
  7.3 59.0 %all-gather.6.cloned.1.call-start = ((), (), s32[]{:S(2)}) async-start(), calls=%async_computation | async-start | bytes 1179648 | tf_op jit(solution)/shard_map/all_gather | solution.py:105
  8.0 109.9 %all-gather.10.cloned.1.call-start = ((), (), s32[]{:S(2)}) async-start(), calls=%async_computation.2 | async-start | bytes 9437184 | tf_op jit(solution)/shard_map/all_gather | solution.py:93
  8.7 165.2 %all-gather.12.cloned.1.call-start = ((), (), s32[]{:S(2)}) async-start(), calls=%async_computation.4 | async-start | bytes 9437184 | tf_op jit(solution)/shard_map/all_gather | solution.py:15
  9.3 352.6 %all-reduce.2.cloned.1.call-start = ((), (), s32[]{:S(2)}) async-start(), calls=%async_computation.3 | async-start | bytes 8388608 | tf_op jit(solution)/shard_map/psum | solution.py:112
  9.4 48.2 %copy-start = (bf16[512,4096]{1,0:T(8,128)(2,1)S(1)}, bf16[512,4096]{1,0:T(8,128)(2,1)}, u32[]{:S(2)}) copy-start(bf16[512,4096]{1,0:T(8,128)(2,1)} %param.10) | copy-start | bytes 12582916
Sparse Core Ops, SparseCore 0:
  9.2 26.7 all-gather.7
  37.9 23.8 all-gather.5
  63.6 54.2 all-gather.9
  119.7 54.2 all-gather.11
  206.9 154.9 all-reduce.1
